TPU v7x, 32 devices: a whole 2x2x4 slice. The times are simulated.
32 devices in a mesh: ctx: 4 (over z), exp: 8 (over y, x, core).
Axes of the slice: x: 2, y: 2, z: 4, core: 2. Of those that a mesh axis runs over, the one named last changes fastest.
Arguments:
- resid_input: bfloat16 [512, 4096], P(('ctx', 'exp')), may hold values from -80 to 80
- norm_gain: float32 [4096], replicated, may hold values from 0.1 to 1.9
- expert_ids: int32 [512, 2], P(('ctx', 'exp')), may hold values from 0 to 3, all different within a row
- route_probs: bfloat16 [512, 2], P(('ctx', 'exp')), may hold values from 0.19921875 to 0.796875
- gate_weight: bfloat16 [8, 6144, 4096], P('exp', 'ctx'), may hold values from -0.09375 to 0.09375
- up_weight: bfloat16 [8, 6144, 4096], P('exp', 'ctx'), may hold values from -0.09375 to 0.09375
- down_weight: bfloat16 [8, 6144, 4096], P('exp', 'ctx'), may hold values from -0.09375 to 0.09375
- grad_output: bfloat16 [512, 4096], P('ctx', 'exp'), may hold values from -6 to 6
- mixer_input: bfloat16 [512, 4096], P('ctx', 'exp'), may hold values from -0.29882812 to 0.29882812
- state_input: bfloat16 [512, 2048], P('ctx', 'exp'), may hold values from -0.5 to 0.5
- state_output: bfloat16 [512, 2048], P('ctx', 'exp'), may hold values from -0.119628906 to 0.119628906
- step_size: float32 [512, 64], P('ctx', 'exp'), may hold values from 0.3 to 1.5
- log_retention: float32 [512, 64], P('ctx', 'exp'), may hold values from -1.5 to 0, as said below
- skip_gain: float32 [64], P('exp'), may hold values from 0.5 to 1.5
Outputs:
- resid_grad: bfloat16 [512, 4096], P('ctx', 'exp')
- mixer_grad: bfloat16 [512, 4096], P('ctx', 'exp')
- state_input_grad: float32 [512, 2048], P('ctx', 'exp')
Inputs may be any that keep to these rules, and one draw needn't show every extreme that they name: `expert_ids`: each token names 2 different experts. `log_retention`: strictly negative.
All inputs are finite; a program needn't handle non-finite values.
Results may differ from a plain program's by a relative error of at most 0.009.
Values may be sent and summed in bfloat16 or wider, within the bound.
No kernel may reach another device: no remote copies, remote signals or barrier semaphores. Data moves between devices by JAX's collectives and lax.ppermute only.
A program may use at most 128 MiB of HBM per device.

v0:
```python
from functools import partial
import jax
import jax.numpy as jnp
from jax import lax
from jax.sharding import PartitionSpec as P

N = 128
highest = lax.Precision.HIGHEST
norm_epsilon = 1e-05


def carried_in(shard, axis, join, neutral):
    count = lax.axis_size(axis)
    place = lax.axis_index(axis)
    ahead = count - 1 - place
    gathered = jax.tree.map(
        lambda a, kind: lax.all_gather(a.astype(kind), axis), shard, (jnp.bfloat16, jnp.bfloat16)
    )
    state = jax.tree.map(lambda a, e: jnp.zeros_like(a) + jnp.asarray(e, a.dtype), shard, neutral)

    def one(hop, state):
        source = count - 1 - hop
        return join(
            state,
            jax.tree.map(
                lambda a, own: lax.dynamic_index_in_dim(a, source, 0, False).astype(own.dtype),
                gathered,
                shard,
            ),
        )

    return lax.fori_loop(0, ahead, one, state)


def expert_slots(flat_ids, expert, capacity):
    matches = (flat_ids == expert).astype(jnp.int32)
    position = jnp.cumsum(matches) - matches
    slot_numbers = jnp.arange(capacity, dtype=jnp.int32)[:, None]
    picked = (position[None, :] == slot_numbers) & (matches[None, :] > 0)
    return picked.astype(jnp.bfloat16)


def mixer_setup(input_states, output_states, log_retention):
    token_count = log_retention.shape[0]
    cumulative = jnp.cumsum(log_retention, axis=0)
    later_mask = jnp.arange(token_count)[None, :] >= jnp.arange(token_count)[:, None]
    difference = cumulative.T[:, None, :] - cumulative.T[:, :, None]
    decay_matrix = jnp.where(
        later_mask[None], jnp.exp(jnp.where(later_mask[None], difference, 0.0)), 0.0
    )
    intersection = jnp.einsum(
        "tgn,sgn->gts", input_states, output_states, preferred_element_type=jnp.float32
    )
    return (cumulative, decay_matrix, intersection)


def mixer_local(
    upstream, inputs_float, step_size, output_float, cumulative, decay_matrix, intersection
):
    token_count, group_count, state_size = output_float.shape
    head_count = upstream.shape[1]
    head_size = upstream.shape[2]
    head_groups = head_count // group_count
    grouped_up = upstream.reshape(token_count, group_count, head_groups, head_size)
    mixed_weights = (
        decay_matrix.reshape(group_count, head_groups, token_count, token_count)
        * intersection[:, None]
    )
    intra_x = jnp.einsum("gjts,sgjp->tgjp", mixed_weights, grouped_up, precision=highest)
    intra_x = intra_x.reshape(token_count, head_count, head_size)
    inner_product = jnp.einsum("thp,shp->hts", inputs_float, upstream, precision=highest)
    weighted = decay_matrix * inner_product * step_size.T[:, :, None]
    grouped = weighted.reshape(group_count, head_groups, token_count, token_count).sum(axis=1)
    intra_b = jnp.einsum("gts,sgn->tgn", grouped, output_float, precision=highest)
    head_decay = jnp.exp(cumulative).reshape(token_count, group_count, head_groups)
    local_state = jnp.einsum(
        "sgj,sgn,sgjp->gjnp", head_decay, output_float, grouped_up, precision=highest
    )
    return (intra_x, intra_b, local_state.reshape(head_count, state_size, head_size))


def chain_combine(earlier, later):
    return (later[0] * earlier[0], later[1] + later[0][:, None, None] * earlier[1])


def body(
    resid_input,
    norm_gain,
    expert_ids,
    route_probs,
    gate_weight,
    up_weight,
    down_weight,
    grad_output,
    mixer_input,
    state_input,
    state_output,
    step_size,
    log_retention,
    skip_gain,
):
    exp_count = lax.axis_size("exp")
    exp_index = lax.axis_index("exp")
    expert_count = exp_count // 2
    token_rows = resid_input.shape[0]
    row_tokens = token_rows * exp_count
    capacity = 2 * row_tokens // expert_count
    model_width = resid_input.shape[1]
    token_count = mixer_input.shape[0]
    head_count = skip_gain.shape[0]
    head_size = mixer_input.shape[1] // head_count
    group_count = state_input.shape[1] // N
    head_groups = head_count // group_count
    input_states = state_input.reshape(token_count, group_count, N)
    output_states = state_output.reshape(token_count, group_count, N)
    input_float = input_states.astype(jnp.float32)
    output_float = output_states.astype(jnp.float32)
    inputs_float = mixer_input.astype(jnp.float32).reshape(token_count, head_count, head_size)
    cumulative, decay_matrix, intersection = mixer_setup(input_states, output_states, log_retention)
    grad_float = grad_output.astype(jnp.float32)
    all_grad = lax.all_gather(grad_output, "exp", axis=1, tiled=True)
    resid_float = resid_input.astype(jnp.float32)
    inverse_rms = lax.rsqrt(
        jnp.mean(resid_float * resid_float, axis=1, keepdims=True) + norm_epsilon
    )
    scaled_input = resid_float * inverse_rms
    normed_rows = (scaled_input * norm_gain[None, :]).astype(jnp.bfloat16)
    all_normed, all_probs = (
        lax.all_gather(normed_rows, "exp", axis=0, tiled=True),
        lax.all_gather(route_probs, "exp", axis=0, tiled=True),
    )
    all_ids = lax.all_gather(expert_ids, "exp", axis=0, tiled=True)
    flat_ids = all_ids.reshape(-1)
    own_expert = exp_index // 2
    selector = expert_slots(flat_ids, own_expert, capacity)
    token_selector = selector.reshape(capacity, row_tokens, 2).sum(axis=2)
    slot_normed = jnp.dot(token_selector, all_normed, preferred_element_type=jnp.float32).astype(
        jnp.bfloat16
    )
    slot_grad = jnp.dot(token_selector, all_grad, preferred_element_type=jnp.float32).astype(
        jnp.bfloat16
    )
    slot_prob = jnp.dot(selector, all_probs.reshape(-1), preferred_element_type=jnp.float32).astype(
        jnp.bfloat16
    )
    rows_normed, rows_grad, rows_prob = (
        lax.all_gather(slot_normed, "ctx", axis=0, tiled=True),
        lax.all_gather(slot_grad, "ctx", axis=0, tiled=True),
        lax.all_gather(slot_prob, "ctx", axis=0, tiled=True),
    )
    gate_rows = gate_weight[0]
    up_rows = up_weight[0]
    down_rows = down_weight[0]
    contract = (((1,), (1,)), ((), ()))
    gate_pre = lax.dot_general(rows_normed, gate_rows, contract, preferred_element_type=jnp.float32)
    up_pre = lax.dot_general(rows_normed, up_rows, contract, preferred_element_type=jnp.float32)
    hidden_grad = lax.dot_general(
        rows_grad, down_rows, contract, preferred_element_type=jnp.float32
    )
    hidden_grad = hidden_grad * rows_prob.astype(jnp.float32)[:, None]
    sigmoid_gate = jax.nn.sigmoid(gate_pre)
    gate_grad = (
        hidden_grad * up_pre * sigmoid_gate * (1.0 + gate_pre * (1.0 - sigmoid_gate))
    ).astype(jnp.bfloat16)
    up_grad = (hidden_grad * gate_pre * sigmoid_gate).astype(jnp.bfloat16)
    half_sum = lax.psum_scatter(
        (
            jnp.dot(gate_grad, gate_rows, preferred_element_type=jnp.float32)
            + jnp.dot(up_grad, up_rows, preferred_element_type=jnp.float32)
        ).astype(jnp.bfloat16),
        "ctx",
        scatter_dimension=0,
        tiled=True,
    ).astype(jnp.float32)
    all_tables = jax.vmap(partial(expert_slots, flat_ids, capacity=capacity))(
        jnp.arange(expert_count, dtype=jnp.int32)
    )
    token_tables = all_tables.reshape(expert_count, capacity, row_tokens, 2).sum(axis=3)
    own_tables = lax.dynamic_slice_in_dim(token_tables, exp_index * token_rows, token_rows, 2)
    parts = lax.all_gather(half_sum.astype(jnp.bfloat16), "exp", axis=0, tiled=True).astype(
        half_sum.dtype
    )
    owner_tables = jnp.repeat(own_tables, 2, axis=0).astype(jnp.float32)
    route_sum = jnp.einsum(
        "xct,xcd->td",
        owner_tables,
        parts.reshape(exp_count, capacity, model_width),
        precision=highest,
    )
    scaled_grad = route_sum * norm_gain[None, :]
    projection = jnp.mean(scaled_grad * scaled_input, axis=1, keepdims=True)
    moe_grad = (inverse_rms * (scaled_grad - scaled_input * projection)).astype(jnp.bfloat16)
    moe_heads = lax.all_to_all(moe_grad, "exp", split_axis=1, concat_axis=0, tiled=True)
    moe_float = moe_heads.astype(jnp.float32)
    upstream = grad_float + moe_float
    resid_grad = upstream.astype(jnp.bfloat16)
    upstream_heads = upstream.reshape(token_count, head_count, head_size)
    intra_x, intra_b, local_state = mixer_local(
        upstream_heads,
        inputs_float,
        step_size,
        output_float,
        cumulative,
        decay_matrix,
        intersection,
    )
    total_decay = jnp.exp(cumulative[-1])
    carried = carried_in(
        (total_decay, local_state),
        "ctx",
        chain_combine,
        (jnp.ones_like(total_decay), jnp.zeros_like(local_state)),
    )
    incoming = carried[1]
    tail_decay = jnp.exp(cumulative[-1][None, :] - cumulative)
    grouped_far = incoming.reshape(group_count, head_groups, N, head_size)
    far_x = jnp.einsum("tgn,gjnp->tgjp", input_float, grouped_far, precision=highest).reshape(
        token_count, head_count, head_size
    )
    far_x = far_x * tail_decay[:, :, None]
    mixer_grad = (
        step_size[:, :, None] * (intra_x + far_x) + skip_gain[None, :, None] * upstream_heads
    )
    mixer_grad = mixer_grad.astype(jnp.bfloat16).reshape(token_count, head_count * head_size)
    far_weight = (inputs_float * (step_size * tail_decay)[:, :, None]).reshape(
        token_count, group_count, head_groups, head_size
    )
    far_b = jnp.einsum("gjnp,tgjp->tgn", grouped_far, far_weight, precision=highest)
    state_input_grad = (intra_b + far_b).reshape(token_count, group_count * N)
    return (resid_grad, mixer_grad, state_input_grad)


def solution(mesh):
    in_specs = (
        P(("ctx", "exp"), None),
        P(),
        P(("ctx", "exp"), None),
        P(("ctx", "exp"), None),
        P("exp", "ctx", None),
        P("exp", "ctx", None),
        P("exp", "ctx", None),
        P("ctx", "exp"),
        P("ctx", "exp"),
        P("ctx", "exp"),
        P("ctx", "exp"),
        P("ctx", "exp"),
        P("ctx", "exp"),
        P("exp"),
    )
    out_specs = (P("ctx", "exp"), P("ctx", "exp"), P("ctx", "exp"))
    return jax.shard_map(body, mesh=mesh, in_specs=in_specs, out_specs=out_specs, check_vma=False)
```

profile of v0, /device:TPU:0, one launch (start us, length us, event | category | flops | bytes accessed | tf_op | source)
XLA Modules:
  0.0 321.4 jit_solution(16942792425635660093)
XLA Ops:
  7.2 1.1 fusion.52
  8.3 1.7 fusion.47
  10.8 10.6 %all-gather = s32[8,16,2]{1,2,0:T(2,128)S(1)} all-gather(s32[1,16,2]{1,2,0:T(2,128)} %bitcast.167), channel_id=1, replica_groups=mesh['ctx'=4,'exp'=8] {'exp'}, dimensions={0}, use_global_device_ids=true | all-gather | bytes 1152 | tf_op jit(solution)/shard_map/all_gather | solution.py:132
  22.7 13.9 %all-gather.13.cloned.1.call-done = bf16[128,4096]{1,0:T(8,128)(2,1)} async-done(((bf16[16,4096]{1,0:T(8,128)(2,1)}), bf16[128,4096]{1,0:T(8,128)(2,1)}) %all-gather.13.cloned.1.call-update) | async-done | bytes 1048592 | tf_op jit(solution)/shard_map/all_gather | solution.py:129
  36.6 2.3 convolution_convert_fusion
  39.0 23.0 %all-gather.9.cloned.1.call-done = bf16[128,4096]{1,0:T(8,128)(2,1)} async-done(((bf16[128,512]{1,0:T(8,128)(2,1)}), bf16[128,4096]{1,0:T(8,128)(2,1)}) %all-gather.9.cloned.1.call-update) | async-done | bytes 1048592 | tf_op jit(solution)/shard_map/all_gather | solution.py:121
  62.0 2.3 convolution_convert_fusion.1
  64.6 8.7 %all-gather.1 = bf16[8,16,2]{1,2,0:T(2,128)(2,1)S(1)} all-gather(bf16[1,16,2]{1,2,0:T(2,128)(2,1)S(1)} %bitcast.169), channel_id=1, replica_groups=mesh['ctx'=4,'exp'=8] {'exp'}, dimensions={0}, use_global_device_ids=true | all-gather | bytes 576 | tf_op jit(solution)/shard_map/all_gather | solution.py:130
  75.3 12.5 %all-reduce = bf16[256]{0:T(256)(128)(2,1)S(1)} all-reduce(bf16[256]{0:T(256)(128)(2,1)S(1)} %dynamic-update-slice), channel_id=1, replica_groups=mesh['ctx'=4,'exp'=8] {'ctx'}, use_global_device_ids=true, to_apply=%add | all-reduce | flops 256 | bytes 1024
  87.8 21.7 %all-gather.15.cloned.1.call-done = bf16[256,4096]{1,0:T(8,128)(2,1)} async-done(((bf16[64,4096]{1,0:T(8,128)(2,1)}), bf16[256,4096]{1,0:T(8,128)(2,1)}) %all-gather.15.cloned.1.call-update) | async-done | bytes 2097168 | tf_op jit(solution)/shard_map/all_gather | solution.py:147
  109.5 9.8 %fusion.2 = f32[256,1536]{1,0:T(8,128)} fusion(bf16[256,4096]{1,0:T(8,128)(2,1)} %all-gather.15.cloned.1.call-done, bf16[1,1536,4096]{2,1,0:T(8,128)(2,1)} %param.20), kind=kOutput, calls=%fused_computation.5 | convolution fusion | flops 3221225472 | bytes 16252928 | tf_op jit(solution)/shard_map/dot_general | solution.py:155
  119.3 36.1 %all-gather.11.cloned.1.call-done = bf16[256,4096]{1,0:T(8,128)(2,1)} async-done(((bf16[64,4096]{1,0:T(8,128)(2,1)}), bf16[256,4096]{1,0:T(8,128)(2,1)}) %all-gather.11.cloned.1.call-update) | async-done | bytes 2097168 | tf_op jit(solution)/shard_map/all_gather | solution.py:148
  155.4 9.9 %fusion.17 = f32[256,1536]{1,0:T(8,128)} fusion(bf16[256,4096]{1,0:T(8,128)(2,1)} %all-gather.11.cloned.1.call-done, bf16[1,1536,4096]{2,1,0:T(8,128)(2,1)} %param.22, f32[256]{0:T(256)S(1)} %convert_element_type.157), kind=kOutput, calls=%fused_computation.19 | convolution fusion | flops 3221618688 | bytes 16253952 | tf_op jit(solution)/shard_map/dot_general | solution.py:157
  165.3 16.3 %fusion = f32[256,4096]{1,0:T(8,128)} fusion(bf16[1,1536,4096]{2,1,0:T(8,128)(2,1)} %param.20, f32[256,1536]{1,0:T(8,128)} %fusion.17, bf16[256,4096]{1,0:T(8,128)(2,1)S(1)} %copy-done.10, bf16[1,1536,4096]{2,1,0:T(8,128)(2,1)} %param.21, f32[256,1536]{1,0:T(8,128)} %fusion.2), kind=kOutput, calls=%fused_computation.3 | convolution fusion | flops 6446383104 | bytes 34603008 | tf_op jit(solution)/shard_map/dot_general | solution.py:168
  181.6 11.5 %fusion.13 = bf16[256,4096]{1,0:T(8,128)(2,1)} fusion(f32[256,4096]{1,0:T(8,128)} %fusion, bf16[1,1536,4096]{2,1,0:T(8,128)(2,1)} %param.21, f32[256,1536]{1,0:T(8,128)} %fusion.17, f32[256,1536]{1,0:T(8,128)} %fusion.2), kind=kOutput, calls=%fused_computation.14 | convolution fusion | flops 3225681920 | bytes 22020096 | tf_op jit(solution)/shard_map/dot_general | solution.py:169
  193.2 42.6 %reduce-scatter.2.cloned.1.call-done = bf16[64,4096]{1,0:T(8,128)(2,1)} async-done(((bf16[256,4096]{1,0:T(8,128)(2,1)}), bf16[64,4096]{1,0:T(8,128)(2,1)}) %reduce-scatter.2.cloned.1.call-update) | async-done | bytes 524304 | tf_op jit(solution)/shard_map/reduce_scatter | solution.py:166
  235.8 1.2 reduce-window.15
  238.7 34.7 %all-gather.17.cloned.1.call-done = bf16[512,4096]{1,0:T(8,128)(2,1)} async-done(((bf16[64,4096]{1,0:T(8,128)(2,1)}), bf16[512,4096]{1,0:T(8,128)(2,1)}) %all-gather.17.cloned.1.call-update) | async-done | bytes 4194320 | tf_op jit(solution)/shard_map/all_gather | solution.py:180
  273.4 3.0 fusion.48
  277.3 3.4 %all-to-all-start = ((bf16[16,8,512]{2,0,1:T(8,128)(2,1)}), bf16[16,8,512]{2,0,1:T(8,128)(2,1)S(1)}, u32[]{:S(2)}, u32[]{:S(2)}) async-start(bf16[16,8,512]{2,0,1:T(8,128)(2,1)} %bitcast.136), calls=%async_computation.1 | async-start | bytes 262144 | tf_op jit(solution)/shard_map/all_to_all | solution.py:193
  280.8 10.9 %all-gather.2 = bf16[4,1,8]{2,1,0:T(2,128)(2,1)S(1)} all-gather(bf16[1,1,8]{2,1,0:T(2,128)(2,1)S(1)} %get-tuple-element.139), channel_id=1, replica_groups=mesh['ctx'=4,'exp'=8] {'ctx'}, dimensions={0}, use_global_device_ids=true | all-gather | bytes 80 | tf_op jit(solution)/shard_map/all_gather | solution.py:17
  293.2 14.9 %all_gather.40 = bf16[4,8,128,64]{2,3,1,0:T(8,128)(2,1)S(1)} all-gather(bf16[1,8,128,64]{2,3,1,0:T(8,128)(2,1)S(1)} %bitcast.153), channel_id=1, replica_groups=mesh['ctx'=4,'exp'=8] {'ctx'}, dimensions={0}, use_global_device_ids=true | all-gather | bytes 655360 | tf_op jit(solution)/shard_map/all_gather | solution.py:17
  308.2 1.2 while.14
  312.4 1.2 fusion.38
  (133 shorter events, 12.8 us)
Async XLA Ops:
  7.2 29.4 %all-gather.13.cloned.1.call-start = ((), (), s32[]{:S(2)}) async-start(), calls=%async_computation.4 | async-start | bytes 1179648 | tf_op jit(solution)/shard_map/all_gather | solution.py:129
  10.0 52.0 %all-gather.9.cloned.1.call-start = ((), (), s32[]{:S(2)}) async-start(), calls=%async_computation.2 | async-start | bytes 1179648 | tf_op jit(solution)/shard_map/all_gather | solution.py:121
  10.7 98.8 %all-gather.15.cloned.1.call-start = ((), (), s32[]{:S(2)}) async-start(), calls=%async_computation.5 | async-start | bytes 2621440 | tf_op jit(solution)/shard_map/all_gather | solution.py:147
  22.6 42.0 %copy-start.8 = (bf16[16,2]{0,1:T(2,128)(2,1)S(1)}, bf16[16,2]{0,1:T(2,128)(2,1)}, u32[]{:S(2)}) copy-start(bf16[16,2]{0,1:T(2,128)(2,1)} %param.19) | copy-start | bytes 196
  22.7 51.0 %copy-start.11 = (u32[32]{0:T(128)S(1)}, u32[32]{0:T(128)}, u32[]{:S(2)}) copy-start(u32[32]{0:T(128)} %constant.95) | copy-start | bytes 388
  38.9 116.5 %all-gather.11.cloned.1.call-start = ((), (), s32[]{:S(2)}) async-start(), calls=%async_computation.3 | async-start | bytes 2621440 | tf_op jit(solution)/shard_map/all_gather | solution.py:148
  64.3 171.5 %reduce-scatter.2.cloned.1.call-start = ((), (), s32[]{:S(2)}) async-start(), calls=%async_computation.6 | async-start | bytes 2621440 | tf_op jit(solution)/shard_map/reduce_scatter | solution.py:166
  119.3 46.0 %copy-start.10 = (bf16[256,4096]{1,0:T(8,128)(2,1)S(1)}, bf16[256,4096]{1,0:T(8,128)(2,1)}, u32[]{:S(2)}) copy-start(bf16[256,4096]{1,0:T(8,128)(2,1)} %all-gather.15.cloned.1.call-done) | copy-start | bytes 6291460
  193.2 44.9 %copy-start.7 = (f32[128,8]{0,1:T(8,128)S(1)}, f32[128,8]{0,1:T(8,128)}, u32[]{:S(2)}) copy-start(f32[128,8]{0,1:T(8,128)} %param.28) | copy-start | bytes 12292
  193.2 45.0 %copy-start.6 = (f32[128,8]{0,1:T(8,128)S(1)}, f32[128,8]{0,1:T(8,128)}, u32[]{:S(2)}) copy-start(f32[128,8]{0,1:T(8,128)} %param.27) | copy-start | bytes 12292
  193.2 45.1 %copy-start.5 = (bf16[128,256]{1,0:T(8,128)(2,1)S(1)}, bf16[128,256]{1,0:T(8,128)(2,1)}, u32[]{:S(2)}) copy-start(bf16[128,256]{1,0:T(8,128)(2,1)} %param.26) | copy-start | bytes 196612
  193.2 80.2 %copy-start = (bf16[16,4096]{1,0:T(8,128)(2,1)S(1)}, bf16[16,4096]{1,0:T(8,128)(2,1)}, u32[]{:S(2)}) copy-start(bf16[16,4096]{1,0:T(8,128)(2,1)} %param.16) | copy-start | bytes 393220
  193.2 80.2 %copy-start.4 = (f32[4096]{0:T(1024)S(1)}, f32[4096]{0:T(1024)}, u32[]{:S(2)}) copy-start(f32[4096]{0:T(1024)} %param.17) | copy-start | bytes 49156
  193.2 80.2 %all-gather.17.cloned.1.call-start = ((), (), s32[]{:S(2)}) async-start(), calls=%async_computation.7 | async-start | bytes 4718592 | tf_op jit(solution)/shard_map/all_gather | solution.py:180
  273.4 7.3 %copy-start.2 = (bf16[128,256]{1,0:T(8,128)(2,1)S(1)}, bf16[128,256]{1,0:T(8,128)(2,1)}, u32[]{:S(2)}) copy-start(bf16[128,256]{1,0:T(8,128)(2,1)} %param.25) | copy-start | bytes 196612
  273.4 18.4 %copy-start.3 = (bf16[128,512]{1,0:T(8,128)(2,1)S(1)}, bf16[128,512]{1,0:T(8,128)(2,1)}, u32[]{:S(2)}) copy-start(bf16[128,512]{1,0:T(8,128)(2,1)} %param.24) | copy-start | bytes 393220
  276.4 16.2 %copy-start.9 = (f32[8]{0:T(128)S(1)}, f32[8]{0:T(128)}, u32[]{:S(2)}) copy-start(f32[8]{0:T(128)} %param.29) | copy-start | bytes 100
  276.4 16.3 %copy-start.1 = (bf16[128,512]{1,0:T(8,128)(2,1)S(1)}, bf16[128,512]{1,0:T(8,128)(2,1)}, u32[]{:S(2)}) copy-start(bf16[128,512]{1,0:T(8,128)(2,1)} %param.23) | copy-start | bytes 393220
  277.3 15.5 %all-to-all-start = ((bf16[16,8,512]{2,0,1:T(8,128)(2,1)}), bf16[16,8,512]{2,0,1:T(8,128)(2,1)S(1)}, u32[]{:S(2)}, u32[]{:S(2)}) async-start(bf16[16,8,512]{2,0,1:T(8,128)(2,1)} %bitcast.136), calls=%async_computation.1 | async-start | bytes 262144 | tf_op jit(solution)/shard_map/all_to_all | solution.py:193
Sparse Core Ops, SparseCore 0:
  10.4 26.1 all-gather.12
  38.5 23.4 all-gather.8
  63.5 45.9 all-gather.14
  110.9 44.4 all-gather.10
  193.3 42.4 reduce-scatter.1
  237.6 35.7 all-gather.16
where the time goes:
time: 322 us; the launch traced here: 321 us
  waiting for transfers between devices  173 us (54%)
  matrix products  59 us (18%)
  blocking collectives  57.6 us (18%)
  between operations  15.2 us (5%)
  local copies, waits for them, and re-layouts  6.84 us (2%)
  other arithmetic  6.27 us (2%)
  starting transfers between devices  3.62 us (1%)
    reduce_scatter x1, waiting for transfers between devices, body(): lax.psum_scatter((jnp.dot(gate_grad, gate_rows, preferred_element_type=jn...  42.6 us
    all_gather x1, waiting for transfers between devices, body(): lax.all_gather(slot_grad, 'ctx', axis=0, tiled=True)  36.1 us
    all_gather x1, waiting for transfers between devices, body(): lax.all_gather(half_sum.astype(jnp.bfloat16), 'exp', axis=0, tiled=True)  34.7 us
    all_gather x2, blocking collectives, carried_in(): lax.all_gather(a.astype(kind), axis)  25.8 us
    all_gather x1, waiting for transfers between devices, body(): all_grad = lax.all_gather(grad_output, 'exp', axis=1, tiled=True)  23 us
    all_gather x1, waiting for transfers between devices, body(): lax.all_gather(slot_normed, 'ctx', axis=0, tiled=True)  21.7 us
    dot_general x1, matrix products, body(): jnp.dot(gate_grad, gate_rows, preferred_element_type=jnp.float32)  16.3 us
    all_gather x1, waiting for transfers between devices, body(): lax.all_gather(normed_rows, 'exp', axis=0, tiled=True)  13.9 us
  transfers between devices with their start and end apart: 7, of which 6 were waited for; matrix products, arithmetic and copies ran while one was open for 7% of the time, Pallas kernels for 0%

commit v1 on v0

--- a/solution.py
+++ b/solution.py
@@ -7,6 +7,22 @@
 N = 128
 highest = lax.Precision.HIGHEST
 norm_epsilon = 1e-05
+
+
+def ring_gather(x, axis, dim):
+    ways, here, hop = (lax.axis_size(axis), lax.axis_index(axis), x.shape[dim])
+    dims = [n * ways if d == dim else n for d, n in enumerate(x.shape)]
+    full = lax.dynamic_update_slice_in_dim(jnp.zeros(dims, x.dtype), x, here * hop, axis=dim)
+    going_up = going_down = x
+    for far in range(1, ways // 2 + 1):
+        going_up = lax.ppermute(going_up, axis, [(d, (d + 1) % ways) for d in range(ways)])
+        full = lax.dynamic_update_slice_in_dim(full, going_up, (here - far) % ways * hop, axis=dim)
+        if 2 * far < ways:
+            going_down = lax.ppermute(going_down, axis, [(d, (d - 1) % ways) for d in range(ways)])
+            full = lax.dynamic_update_slice_in_dim(
+                full, going_down, (here + far) % ways * hop, axis=dim
+            )
+    return full
 
 
 def carried_in(shard, axis, join, neutral):
@@ -177,9 +193,7 @@
     )
     token_tables = all_tables.reshape(expert_count, capacity, row_tokens, 2).sum(axis=3)
     own_tables = lax.dynamic_slice_in_dim(token_tables, exp_index * token_rows, token_rows, 2)
-    parts = lax.all_gather(half_sum.astype(jnp.bfloat16), "exp", axis=0, tiled=True).astype(
-        half_sum.dtype
-    )
+    parts = ring_gather(half_sum.astype(jnp.bfloat16), "exp", 0).astype(half_sum.dtype)
     owner_tables = jnp.repeat(own_tables, 2, axis=0).astype(jnp.float32)
     route_sum = jnp.einsum(
         "xct,xcd->td",

time: 322 us -> 333 us (1.034)
  starting transfers between devices: 3.62 us -> 12.6 us
  waiting for transfers between devices: 173 us -> 178 us
    ppermute x0 -> x7, waiting for transfers between devices: none -> 42.3 us  [the longest x4 42.3 us: ring_gather(): lax.ppermute(going_up, axis, [(d, (d + 1) % ways) for d in range(ways)])]
    all_gather x1 -> x0, waiting for transfers between devices: 34.7 us -> none  [body(): lax.all_gather(half_sum.astype(jnp.bfloat16), 'exp', axis=0, tiled=True)]
    ppermute x0 -> x7, starting transfers between devices: none -> 7.95 us  [the longest x3 7.94 us: ring_gather(): lax.ppermute(going_down, axis, [(d, (d - 1) % ways) for d in range(ways)])]
  transfers between devices with their start and end apart: 7 -> 13, of which waited for: 6 -> 9; matrix products, arithmetic and copies ran while one was open for 7% -> 7% of each run, Pallas kernels for 0% -> 0%
where the time goes in v1:
time: 333 us
  waiting for transfers between devices  178 us (53%)
  matrix products  56.8 us (17%)
  blocking collectives  56.3 us (17%)
  between operations  15.1 us (5%)
  starting transfers between devices  12.6 us (4%)
  local copies, waits for them, and re-layouts  7.65 us (2%)
  other arithmetic  6.27 us (2%)
    ppermute x4, waiting for transfers between devices, ring_gather(): lax.ppermute(going_up, axis, [(d, (d + 1) % ways) for d in range(ways)])  42.3 us
    reduce_scatter x1, waiting for transfers between devices, body(): lax.psum_scatter((jnp.dot(gate_grad, gate_rows, preferred_element_type=jn...  40 us
    all_gather x1, waiting for transfers between devices, body(): lax.all_gather(slot_grad, 'ctx', axis=0, tiled=True)  36.1 us
    all_gather x2, blocking collectives, carried_in(): lax.all_gather(a.astype(kind), axis)  24.6 us
    all_gather x1, waiting for transfers between devices, body(): all_grad = lax.all_gather(grad_output, 'exp', axis=1, tiled=True)  23 us
    all_gather x1, waiting for transfers between devices, body(): lax.all_gather(slot_normed, 'ctx', axis=0, tiled=True)  21.7 us
    dot_general x1, matrix products, body(): jnp.dot(gate_grad, gate_rows, preferred_element_type=jnp.float32)  16.3 us
    all_gather x1, waiting for transfers between devices, body(): lax.all_gather(normed_rows, 'exp', axis=0, tiled=True)  13.9 us
  transfers between devices with their start and end apart: 13, of which 9 were waited for; matrix products, arithmetic and copies ran while one was open for 7% of the time, Pallas kernels for 0%

profile of v1, /device:TPU:0, one launch (start us, length us, event | category | flops | bytes accessed | tf_op | source)
XLA Modules:
  0.0 332.7 jit_solution(12296967862989923678)
XLA Ops:
  10.8 10.6 %all-gather = s32[8,16,2]{1,2,0:T(2,128)S(1)} all-gather(s32[1,16,2]{1,2,0:T(2,128)} %bitcast.167), channel_id=1, replica_groups=mesh['ctx'=4,'exp'=8] {'exp'}, dimensions={0}, use_global_device_ids=true | all-gather | bytes 1152 | tf_op jit(solution)/shard_map/all_gather | solution.py:148
  22.7 13.9 %all-gather.12.cloned.1.call-done = bf16[128,4096]{1,0:T(8,128)(2,1)} async-done(((bf16[16,4096]{1,0:T(8,128)(2,1)}), bf16[128,4096]{1,0:T(8,128)(2,1)}) %all-gather.12.cloned.1.call-update) | async-done | bytes 1048592 | tf_op jit(solution)/shard_map/all_gather | solution.py:145
  36.6 2.3 convolution_convert_fusion
  39.0 23.0 %all-gather.8.cloned.1.call-done = bf16[128,4096]{1,0:T(8,128)(2,1)} async-done(((bf16[128,512]{1,0:T(8,128)(2,1)}), bf16[128,4096]{1,0:T(8,128)(2,1)}) %all-gather.8.cloned.1.call-update) | async-done | bytes 1048592 | tf_op jit(solution)/shard_map/all_gather | solution.py:137
  62.0 2.3 convolution_convert_fusion.1
  64.7 8.7 %all-gather.1 = bf16[8,16,2]{1,2,0:T(2,128)(2,1)S(1)} all-gather(bf16[1,16,2]{1,2,0:T(2,128)(2,1)S(1)} %bitcast.169), channel_id=1, replica_groups=mesh['ctx'=4,'exp'=8] {'exp'}, dimensions={0}, use_global_device_ids=true | all-gather | bytes 576 | tf_op jit(solution)/shard_map/all_gather | solution.py:146
  75.4 12.4 %all-reduce = bf16[256]{0:T(256)(128)(2,1)S(1)} all-reduce(bf16[256]{0:T(256)(128)(2,1)S(1)} %dynamic-update-slice), channel_id=1, replica_groups=mesh['ctx'=4,'exp'=8] {'ctx'}, use_global_device_ids=true, to_apply=%add | all-reduce | flops 256 | bytes 1024
  87.8 21.7 %all-gather.14.cloned.1.call-done = bf16[256,4096]{1,0:T(8,128)(2,1)} async-done(((bf16[64,4096]{1,0:T(8,128)(2,1)}), bf16[256,4096]{1,0:T(8,128)(2,1)}) %all-gather.14.cloned.1.call-update) | async-done | bytes 2097168 | tf_op jit(solution)/shard_map/all_gather | solution.py:163
  109.5 9.8 %fusion.2 = f32[256,1536]{1,0:T(8,128)} fusion(bf16[256,4096]{1,0:T(8,128)(2,1)} %all-gather.14.cloned.1.call-done, bf16[1,1536,4096]{2,1,0:T(8,128)(2,1)} %param.20), kind=kOutput, calls=%fused_computation.5 | convolution fusion | flops 3221225472 | bytes 16252928 | tf_op jit(solution)/shard_map/dot_general | solution.py:171
  119.3 36.1 %all-gather.10.cloned.1.call-done = bf16[256,4096]{1,0:T(8,128)(2,1)} async-done(((bf16[64,4096]{1,0:T(8,128)(2,1)}), bf16[256,4096]{1,0:T(8,128)(2,1)}) %all-gather.10.cloned.1.call-update) | async-done | bytes 2097168 | tf_op jit(solution)/shard_map/all_gather | solution.py:164
  155.4 9.9 %fusion.17 = f32[256,1536]{1,0:T(8,128)} fusion(bf16[256,4096]{1,0:T(8,128)(2,1)} %all-gather.10.cloned.1.call-done, bf16[1,1536,4096]{2,1,0:T(8,128)(2,1)} %param.22, f32[256]{0:T(256)S(1)} %convert_element_type.157), kind=kOutput, calls=%fused_computation.19 | convolution fusion | flops 3221618688 | bytes 16253952 | tf_op jit(solution)/shard_map/dot_general | solution.py:173
  165.3 16.3 %fusion = f32[256,4096]{1,0:T(8,128)} fusion(bf16[1,1536,4096]{2,1,0:T(8,128)(2,1)} %param.20, f32[256,1536]{1,0:T(8,128)} %fusion.17, bf16[256,4096]{1,0:T(8,128)(2,1)S(1)} %copy-done.11, bf16[1,1536,4096]{2,1,0:T(8,128)(2,1)} %param.21, f32[256,1536]{1,0:T(8,128)} %fusion.2), kind=kOutput, calls=%fused_computation.3 | convolution fusion | flops 6446383104 | bytes 34603008 | tf_op jit(solution)/shard_map/dot_general | solution.py:184
  181.7 11.5 %fusion.13 = bf16[256,4096]{1,0:T(8,128)(2,1)} fusion(f32[256,4096]{1,0:T(8,128)} %fusion, bf16[1,1536,4096]{2,1,0:T(8,128)(2,1)} %param.21, f32[256,1536]{1,0:T(8,128)} %fusion.17, f32[256,1536]{1,0:T(8,128)} %fusion.2), kind=kOutput, calls=%fused_computation.14 | convolution fusion | flops 3225681920 | bytes 22020096 | tf_op jit(solution)/shard_map/dot_general | solution.py:185
  195.8 40.0 %reduce-scatter.2.cloned.1.call-done = bf16[64,4096]{1,0:T(8,128)(2,1)} async-done(((bf16[256,4096]{1,0:T(8,128)(2,1)}), bf16[64,4096]{1,0:T(8,128)(2,1)}) %reduce-scatter.2.cloned.1.call-update) | async-done | bytes 524304 | tf_op jit(solution)/shard_map/reduce_scatter | solution.py:182
  235.8 2.6 collective-permute-start.1
  239.4 9.9 %collective-permute-done = bf16[64,4096]{1,0:T(8,128)(2,1)S(1)} collective-permute-done((bf16[64,4096]{1,0:T(8,128)(2,1)}, bf16[64,4096]{1,0:T(8,128)(2,1)S(1)}, u32[]{:S(2)}, u32[]{:S(2)}) %collective-permute-start) | collective-permute-done | bytes 524320 | tf_op jit(solution)/shard_map/ppermute | solution.py:18
  249.4 2.7 collective-permute-start.3
  252.1 11.2 %collective-permute-done.2 = bf16[64,4096]{1,0:T(8,128)(2,1)S(1)} collective-permute-done((bf16[64,4096]{1,0:T(8,128)(2,1)S(1)}, bf16[64,4096]{1,0:T(8,128)(2,1)S(1)}, u32[]{:S(2)}, u32[]{:S(2)}) %collective-permute-start.2) | collective-permute-done | bytes 524320 | tf_op jit(solution)/shard_map/ppermute | solution.py:18
  263.3 2.6 collective-permute-start.5
  266.1 11.8 %collective-permute-done.4 = bf16[64,4096]{1,0:T(8,128)(2,1)S(1)} collective-permute-done((bf16[64,4096]{1,0:T(8,128)(2,1)S(1)}, bf16[64,4096]{1,0:T(8,128)(2,1)S(1)}, u32[]{:S(2)}, u32[]{:S(2)}) %collective-permute-start.4) | collective-permute-done | bytes 524320 | tf_op jit(solution)/shard_map/ppermute | solution.py:18
  278.0 9.4 %collective-permute-done.6 = bf16[64,4096]{1,0:T(8,128)(2,1)S(1)} collective-permute-done((bf16[64,4096]{1,0:T(8,128)(2,1)S(1)}, bf16[64,4096]{1,0:T(8,128)(2,1)S(1)}, u32[]{:S(2)}, u32[]{:S(2)}) %collective-permute-start.6) | collective-permute-done | bytes 524320 | tf_op jit(solution)/shard_map/ppermute | solution.py:18
  289.1 4.4 %all-to-all-start = ((bf16[16,8,512]{2,0,1:T(8,128)(2,1)}), bf16[16,8,512]{2,0,1:T(8,128)(2,1)S(1)}, u32[]{:S(2)}, u32[]{:S(2)}) async-start(bf16[16,8,512]{2,0,1:T(8,128)(2,1)} %bitcast.136), calls=%async_computation.1 | async-start | bytes 262144 | tf_op jit(solution)/shard_map/all_to_all | solution.py:207
  293.7 9.4 %all-gather.2 = bf16[4,1,8]{2,1,0:T(2,128)(2,1)S(1)} all-gather(bf16[1,1,8]{2,1,0:T(2,128)(2,1)S(1)} %get-tuple-element.139), channel_id=1, replica_groups=mesh['ctx'=4,'exp'=8] {'ctx'}, dimensions={0}, use_global_device_ids=true | all-gather | bytes 80 | tf_op jit(solution)/shard_map/all_gather | solution.py:33
  304.6 15.2 %all_gather.36 = bf16[4,8,128,64]{2,3,1,0:T(8,128)(2,1)S(1)} all-gather(bf16[1,8,128,64]{2,3,1,0:T(8,128)(2,1)S(1)} %bitcast.153), channel_id=1, replica_groups=mesh['ctx'=4,'exp'=8] {'ctx'}, dimensions={0}, use_global_device_ids=true | all-gather | bytes 655360 | tf_op jit(solution)/shard_map/all_gather | solution.py:33
  (155 shorter events, 20.7 us)
Async XLA Ops:
  7.2 66.5 %copy-start.12 = (u32[32]{0:T(128)S(1)}, u32[32]{0:T(128)}, u32[]{:S(2)}) copy-start(u32[32]{0:T(128)} %constant.146) | copy-start | bytes 388
  7.2 57.5 %copy-start.9 = (bf16[16,2]{0,1:T(2,128)(2,1)S(1)}, bf16[16,2]{0,1:T(2,128)(2,1)}, u32[]{:S(2)}) copy-start(bf16[16,2]{0,1:T(2,128)(2,1)} %param.19) | copy-start | bytes 196
  7.2 29.4 %all-gather.12.cloned.1.call-start = ((), (), s32[]{:S(2)}) async-start(), calls=%async_computation.4 | async-start | bytes 1179648 | tf_op jit(solution)/shard_map/all_gather | solution.py:145
  10.0 52.0 %all-gather.8.cloned.1.call-start = ((), (), s32[]{:S(2)}) async-start(), calls=%async_computation.2 | async-start | bytes 1179648 | tf_op jit(solution)/shard_map/all_gather | solution.py:137
  10.7 98.8 %all-gather.14.cloned.1.call-start = ((), (), s32[]{:S(2)}) async-start(), calls=%async_computation.5 | async-start | bytes 2621440 | tf_op jit(solution)/shard_map/all_gather | solution.py:163
  39.0 116.5 %all-gather.10.cloned.1.call-start = ((), (), s32[]{:S(2)}) async-start(), calls=%async_computation.3 | async-start | bytes 2621440 | tf_op jit(solution)/shard_map/all_gather | solution.py:164
  64.3 171.5 %reduce-scatter.2.cloned.1.call-start = ((), (), s32[]{:S(2)}) async-start(), calls=%async_computation.6 | async-start | bytes 2621440 | tf_op jit(solution)/shard_map/reduce_scatter | solution.py:182
  119.3 46.0 %copy-start.11 = (bf16[256,4096]{1,0:T(8,128)(2,1)S(1)}, bf16[256,4096]{1,0:T(8,128)(2,1)}, u32[]{:S(2)}) copy-start(bf16[256,4096]{1,0:T(8,128)(2,1)} %all-gather.14.cloned.1.call-done) | copy-start | bytes 6291460
  181.6 13.8 %copy-start.7 = (f32[128,8]{0,1:T(8,128)S(1)}, f32[128,8]{0,1:T(8,128)}, u32[]{:S(2)}) copy-start(f32[128,8]{0,1:T(8,128)} %param.27) | copy-start | bytes 12292
  181.6 57.0 %copy-start.6 = (bf16[128,256]{1,0:T(8,128)(2,1)S(1)}, bf16[128,256]{1,0:T(8,128)(2,1)}, u32[]{:S(2)}) copy-start(bf16[128,256]{1,0:T(8,128)(2,1)} %param.26) | copy-start | bytes 196612
  235.8 13.6 %collective-permute-start = (bf16[64,4096]{1,0:T(8,128)(2,1)}, bf16[64,4096]{1,0:T(8,128)(2,1)S(1)}, u32[]{:S(2)}, u32[]{:S(2)}) collective-permute-start(bf16[64,4096]{1,0:T(8,128)(2,1)} %reduce-scatter.2.cloned.1.call-done), channel_id=1, source_target_pairs={{0,1},{1,2},{2,3},{3,4},{4,5},{5,6},{6,7},{7,0},{8,9},{9,10},{10,1... | collective-permute-start | bytes 1572872 | tf_op jit(solution)/shard_map/ppermute | solution.py:18
  235.8 13.6 %collective-permute-start.1 = (bf16[64,4096]{1,0:T(8,128)(2,1)}, bf16[64,4096]{1,0:T(8,128)(2,1)S(1)}, u32[]{:S(2)}, u32[]{:S(2)}) collective-permute-start(bf16[64,4096]{1,0:T(8,128)(2,1)} %reduce-scatter.2.cloned.1.call-done), channel_id=1, source_target_pairs={{0,7},{1,0},{2,1},{3,2},{4,3},{5,4},{6,5},{7,6},{8,15},{9,8},{10,9... | collective-permute-start | bytes 1572872 | tf_op jit(solution)/shard_map/ppermute | solution.py:21
  239.4 48.1 %copy-start = (bf16[16,4096]{1,0:T(8,128)(2,1)S(1)}, bf16[16,4096]{1,0:T(8,128)(2,1)}, u32[]{:S(2)}) copy-start(bf16[16,4096]{1,0:T(8,128)(2,1)} %param.16) | copy-start | bytes 393220
  239.4 48.1 %copy-start.5 = (f32[4096]{0:T(1024)S(1)}, f32[4096]{0:T(1024)}, u32[]{:S(2)}) copy-start(f32[4096]{0:T(1024)} %param.17) | copy-start | bytes 49156
  249.4 13.9 %collective-permute-start.2 = (bf16[64,4096]{1,0:T(8,128)(2,1)S(1)}, bf16[64,4096]{1,0:T(8,128)(2,1)S(1)}, u32[]{:S(2)}, u32[]{:S(2)}) collective-permute-start(bf16[64,4096]{1,0:T(8,128)(2,1)S(1)} %collective-permute-done), channel_id=1, source_target_pairs={{0,1},{1,2},{2,3},{3,4},{4,5},{5,6},{6,7},{7,0},{8,9},{9,10},{10,1... | collective-permute-start | bytes 1572872 | tf_op jit(solution)/shard_map/ppermute | solution.py:18
  249.4 13.9 %collective-permute-start.3 = (bf16[64,4096]{1,0:T(8,128)(2,1)S(1)}, bf16[64,4096]{1,0:T(8,128)(2,1)S(1)}, u32[]{:S(2)}, u32[]{:S(2)}) collective-permute-start(bf16[64,4096]{1,0:T(8,128)(2,1)S(1)} %collective-permute-done.1), channel_id=1, source_target_pairs={{0,7},{1,0},{2,1},{3,2},{4,3},{5,4},{6,5},{7,6},{8,15},{9,8},{10,9... | collective-permute-start | bytes 1572872 | tf_op jit(solution)/shard_map/ppermute | solution.py:21
  263.3 14.6 %collective-permute-start.4 = (bf16[64,4096]{1,0:T(8,128)(2,1)S(1)}, bf16[64,4096]{1,0:T(8,128)(2,1)S(1)}, u32[]{:S(2)}, u32[]{:S(2)}) collective-permute-start(bf16[64,4096]{1,0:T(8,128)(2,1)S(1)} %collective-permute-done.2), channel_id=1, source_target_pairs={{0,1},{1,2},{2,3},{3,4},{4,5},{5,6},{6,7},{7,0},{8,9},{9,10},{10,1... | collective-permute-start | bytes 1572872 | tf_op jit(solution)/shard_map/ppermute | solution.py:18
  263.3 14.6 %collective-permute-start.5 = (bf16[64,4096]{1,0:T(8,128)(2,1)S(1)}, bf16[64,4096]{1,0:T(8,128)(2,1)S(1)}, u32[]{:S(2)}, u32[]{:S(2)}) collective-permute-start(bf16[64,4096]{1,0:T(8,128)(2,1)S(1)} %collective-permute-done.3), channel_id=1, source_target_pairs={{0,7},{1,0},{2,1},{3,2},{4,3},{5,4},{6,5},{7,6},{8,15},{9,8},{10,9... | collective-permute-start | bytes 1572872 | tf_op jit(solution)/shard_map/ppermute | solution.py:21
  266.1 27.5 %copy-start.3 = (bf16[128,256]{1,0:T(8,128)(2,1)S(1)}, bf16[128,256]{1,0:T(8,128)(2,1)}, u32[]{:S(2)}) copy-start(bf16[128,256]{1,0:T(8,128)(2,1)} %param.25) | copy-start | bytes 196612
  277.9 9.5 %collective-permute-start.6 = (bf16[64,4096]{1,0:T(8,128)(2,1)S(1)}, bf16[64,4096]{1,0:T(8,128)(2,1)S(1)}, u32[]{:S(2)}, u32[]{:S(2)}) collective-permute-start(bf16[64,4096]{1,0:T(8,128)(2,1)S(1)} %collective-permute-done.4), channel_id=1, source_target_pairs={{0,1},{1,2},{2,3},{3,4},{4,5},{5,6},{6,7},{7,0},{8,9},{9,10},{10,1... | collective-permute-start | bytes 1572872 | tf_op jit(solution)/shard_map/ppermute | solution.py:18
  277.9 25.3 %copy-start.4 = (bf16[128,512]{1,0:T(8,128)(2,1)S(1)}, bf16[128,512]{1,0:T(8,128)(2,1)}, u32[]{:S(2)}) copy-start(bf16[128,512]{1,0:T(8,128)(2,1)} %param.24) | copy-start | bytes 393220
  287.4 16.6 %copy-start.10 = (f32[8]{0:T(128)S(1)}, f32[8]{0:T(128)}, u32[]{:S(2)}) copy-start(f32[8]{0:T(128)} %param.29) | copy-start | bytes 100
  287.4 16.7 %copy-start.1 = (bf16[128,512]{1,0:T(8,128)(2,1)S(1)}, bf16[128,512]{1,0:T(8,128)(2,1)}, u32[]{:S(2)}) copy-start(bf16[128,512]{1,0:T(8,128)(2,1)} %param.23) | copy-start | bytes 393220
  289.1 15.1 %all-to-all-start = ((bf16[16,8,512]{2,0,1:T(8,128)(2,1)}), bf16[16,8,512]{2,0,1:T(8,128)(2,1)S(1)}, u32[]{:S(2)}, u32[]{:S(2)}) async-start(bf16[16,8,512]{2,0,1:T(8,128)(2,1)} %bitcast.136), calls=%async_computation.1 | async-start | bytes 262144 | tf_op jit(solution)/shard_map/all_to_all | solution.py:207
  (2 other events, 17.2 us)
Sparse Core Ops, SparseCore 0:
  10.5 26.1 all-gather.11
  38.5 23.4 all-gather.7
  63.6 45.9 all-gather.13
  110.9 44.4 all-gather.9
  193.3 42.4 reduce-scatter.1
